TPU v7x, 768 devices: a whole 4x8x12 slice. The times are simulated.
768 devices in a mesh: sx: 192 (over z, y, core), sy: 4 (over x).
Axes of the slice: x: 4, y: 8, z: 12, core: 2. Of those that a mesh axis runs over, the one named last changes fastest.
Arguments:
- flexibility: bfloat16 [192, 4, 1536, 1536], P('sx', 'sy'), as said below
- loads: bfloat16 [192, 4, 36, 1536], P('sx', 'sy'), may hold values from -32 to 32
- face_sizes: int32 [192, 4, 2], replicated, may hold values from 96 to 384, as said below
- face_owner: int32 [192, 4, 2], replicated, may hold values from 0 to 1
Outputs:
- multipliers: bfloat16 [192, 4, 2, 36, 384], P('sx', 'sy')
Inputs may be any that keep to these rules, and one draw needn't show every extreme that they name: `flexibility`: each matrix is symmetric positive definite. Slots 0 to face_sizes - 1 of a face are live; entries for the grid's last row (index 0) or last column (index 1) are unused; some face has 384 live slots. `face_owner`: 0: the subdomain with the lower index carries the plus sign.
All inputs are finite; a program needn't handle non-finite values.
Results may differ from a plain program's by a relative error of at most 0.0044.
Values may be sent and summed in bfloat16 or wider, within the bound.
A program may use at most 32 MiB of HBM per device.

v0:
```python
import jax
import jax.numpy as jnp
from jax import lax
from jax.sharding import PartitionSpec as P

FACE = 384
ITERS = 2


def passed_along(value, axis, steps):
    count = lax.axis_size(axis)
    initial, last = (max(0, -steps), min(count, count - steps))
    return lax.ppermute(value, axis, [(source, source + steps) for source in range(initial, last)])


def face_coefficient(face_sizes, face_owner, row_index, col_index, face_kind, present):
    safe_row = jnp.clip(row_index, 0, face_sizes.shape[0] - 1)
    safe_col = jnp.clip(col_index, 0, face_sizes.shape[1] - 1)
    live_count = face_sizes[safe_row, safe_col, face_kind]
    owner_sign = (1 - 2 * face_owner[safe_row, safe_col, face_kind]).astype(jnp.float32)
    live_mask = (jnp.arange(FACE, dtype=jnp.int32) < live_count) & present
    return jnp.where(live_mask, owner_sign, jnp.float32(0.0))


def global_total(partial_value):
    return lax.psum(partial_value, ("sx", "sy"))


def body(flexibility, loads, face_sizes, face_owner):
    flex_matrix = flexibility[0, 0]
    forces = loads[0, 0]
    grid_rows = lax.axis_size("sx")
    grid_cols = lax.axis_size("sy")
    my_row = lax.axis_index("sx")
    my_col = lax.axis_index("sy")
    high_x = face_coefficient(face_sizes, face_owner, my_row, my_col, 0, my_row < grid_rows - 1)
    high_y = face_coefficient(face_sizes, face_owner, my_row, my_col, 1, my_col < grid_cols - 1)
    coef_high = jnp.stack([high_x, high_y])[:, None, :]

    def operate(search, is_first):
        if is_first:
            pushed = forces
        else:
            sent_faces = (coef_high * search).astype(jnp.bfloat16)
            from_below = passed_along(sent_faces[0], "sx", 1)
            from_left = passed_along(sent_faces[1], "sy", 1)
            pushed = jnp.concatenate(
                [-from_below, sent_faces[0], -from_left, sent_faces[1]], axis=1
            )
        images = jnp.dot(pushed, flex_matrix, preferred_element_type=jnp.float32)
        from_above = passed_along(images[:, 0:FACE], "sx", -1)
        from_right = passed_along(images[:, 2 * FACE : 3 * FACE], "sy", -1)
        differences = jnp.stack(
            [images[:, FACE : 2 * FACE] - from_above, images[:, 3 * FACE : 4 * FACE] - from_right]
        )
        return coef_high * differences

    def own_total(first_factor, second_factor):
        return jnp.sum(first_factor * second_factor, axis=(0, 2))

    def per_load(values):
        return values[None, :, None]

    right_side = operate(None, True)
    residual = right_side
    search = right_side
    multipliers = jnp.zeros_like(right_side)
    norm_now = global_total(own_total(residual, residual))
    for iteration in range(ITERS):
        image_now = operate(search, False)
        step_size = per_load(norm_now / global_total(own_total(search, image_now)))
        multipliers = multipliers + step_size * search
        residual = residual - step_size * image_now
        if iteration + 1 < ITERS:
            norm_next = global_total(own_total(residual, residual))
            search = residual + per_load(norm_next / norm_now) * search
            norm_now = norm_next
    return multipliers.astype(jnp.bfloat16)[None, None]


def solution(mesh):
    return jax.shard_map(
        body,
        mesh=mesh,
        in_specs=(P("sx", "sy", None, None), P("sx", "sy", None, None), P(), P()),
        out_specs=P("sx", "sy", None, None, None),
        check_vma=False,
    )
```

profile of v0, /device:TPU:1, one launch (start us, length us, event | category | flops | bytes accessed | tf_op | source)
XLA Modules:
  0.0 396.9 jit_solution(8378505877259201758)
XLA Ops:
  0.0 0.0 copy-start
  0.0 0.9 copy-done
  0.9 3.2 fusion.4
  4.2 12.4 %collective-permute-start = (f32[36,384]{1,0:T(8,128)S(1)}, f32[36,384]{1,0:T(8,128)S(1)}, u32[]{:S(2)}, u32[]{:S(2)}) collective-permute-start(f32[36,384]{1,0:T(8,128)S(1)} %get-tuple-element.24), channel_id=1, source_target_pairs={{4,0},{8,4},{12,8},{16,12},{20,16},{24,20},{28,24},{32,28},{36,32}... | collective-permute-start | bytes 165896 | tf_op jit(solution)/shard_map/ppermute | solution.py:13
  16.6 1.3 collective-permute-start.1
  17.9 1.4 constant_dynamic-slice_fusion.2
  20.6 0.6 and_select_fusion.1
  21.2 0.6 and_select_fusion
  21.9 0.0 collective-permute-done
  21.9 0.3 collective-permute-done.1
  22.2 1.9 collective-permute-start.2
  24.2 3.7 collective-permute-start.3
  27.9 0.0 collective-permute-done.2
  27.9 1.0 collective-permute-done.3
  28.9 3.2 fusion.2
  32.1 3.3 collective-permute-start.4
  35.4 2.3 collective-permute-done.4
  37.7 1.3 collective-permute-start.5
  39.0 4.0 %collective-permute-done.5 = f32[36,384]{1,0:T(8,128)S(1)} collective-permute-done((f32[36,384]{1,0:T(8,128)S(1)}, f32[36,384]{1,0:T(8,128)S(1)}, u32[]{:S(2)}, u32[]{:S(2)}) %collective-permute-start.5) | collective-permute-done | bytes 55328 | tf_op jit(solution)/shard_map/ppermute | solution.py:13
  43.1 0.1 multiply_reduce_fusion.1
  43.2 116.0 %all-reduce = (f32[36]{0:T(128)S(1)}, f32[36]{0:T(128)S(1)}) all-reduce(f32[36]{0:T(128)S(1)} %get-tuple-element.6, f32[36]{0:T(128)S(1)} %get-tuple-element.5), channel_id=1, replica_groups=mesh['sx'=192,'sy'=4] {'sx','sy'}, use_global_device_ids=true, to_apply=%region_1.2 | all-reduce | flops 72 | bytes 576 | tf_op jit(solution)/shard_map/psum | solution.py:26
  159.2 0.2 multiply_reduce_fusion
  159.3 104.3 %psum.30 = f32[36]{0:T(128)S(1)} all-reduce(f32[36]{0:T(128)S(1)} %multiply_reduce_fusion), channel_id=1, replica_groups=mesh['sx'=192,'sy'=4] {'sx','sy'}, use_global_device_ids=true, to_apply=%region_5.6 | all-reduce | flops 36 | bytes 288 | tf_op jit(solution)/shard_map/psum | solution.py:26
  263.6 0.1 multiply_convert_fusion
  263.8 1.9 collective-permute-start.6
  265.7 3.1 collective-permute-start.7
  268.8 0.0 collective-permute-done.6
  268.8 1.0 collective-permute-done.7
  269.7 3.2 fusion
  273.0 3.3 collective-permute-start.8
  276.3 2.3 collective-permute-done.8
  278.6 1.3 collective-permute-start.9
  279.9 4.0 %collective-permute-done.9 = f32[36,384]{1,0:T(8,128)S(1)} collective-permute-done((f32[36,384]{1,0:T(8,128)S(1)}, f32[36,384]{1,0:T(8,128)S(1)}, u32[]{:S(2)}, u32[]{:S(2)}) %collective-permute-start.9) | collective-permute-done | bytes 55328 | tf_op jit(solution)/shard_map/ppermute | solution.py:13
  283.9 0.1 fusion.21
  284.0 112.1 %psum.31 = f32[36]{0:T(128)S(1)} all-reduce(f32[36]{0:T(128)S(1)} %fusion.21), channel_id=1, replica_groups=mesh['sx'=192,'sy'=4] {'sx','sy'}, use_global_device_ids=true, to_apply=%region_7.8 | all-reduce | flops 36 | bytes 288 | tf_op jit(solution)/shard_map/psum | solution.py:26
  396.1 0.1 fusion.27
  396.3 0.7 copy.5
  (19 shorter events, 0.2 us)
Async XLA Ops:
  0.0 0.9 copy-start
  4.2 17.7 %collective-permute-start = (f32[36,384]{1,0:T(8,128)S(1)}, f32[36,384]{1,0:T(8,128)S(1)}, u32[]{:S(2)}, u32[]{:S(2)}) collective-permute-start(f32[36,384]{1,0:T(8,128)S(1)} %get-tuple-element.24), channel_id=1, source_target_pairs={{4,0},{8,4},{12,8},{16,12},{20,16},{24,20},{28,24},{32,28},{36,32}... | collective-permute-start | bytes 165896 | tf_op jit(solution)/shard_map/ppermute | solution.py:13
  16.6 5.6 %collective-permute-start.1 = (f32[36,384]{1,0:T(8,128)S(1)}, f32[36,384]{1,0:T(8,128)S(1)}, u32[]{:S(2)}, u32[]{:S(2)}) collective-permute-start(f32[36,384]{1,0:T(8,128)S(1)} %get-tuple-element.25), channel_id=1, source_target_pairs={{1,0},{2,1},{3,2},{5,4},{6,5},{7,6},{9,8},{10,9},{11,10},{13,12},{... | collective-permute-start | bytes 165896 | tf_op jit(solution)/shard_map/ppermute | solution.py:13
  22.2 5.7 %collective-permute-start.2 = (bf16[36,384]{1,0:T(8,128)(2,1)S(1)}, bf16[36,384]{1,0:T(8,128)(2,1)S(1)}, u32[]{:S(2)}, u32[]{:S(2)}) collective-permute-start(bf16[36,384]{1,0:T(8,128)(2,1)S(1)} %get-tuple-element.28), channel_id=1, source_target_pairs={{0,4},{4,8},{8,12},{12,16},{16,20},{20,24},{24,28},{28,32},{32,36}... | collective-permute-start | bytes 82952 | tf_op jit(solution)/shard_map/ppermute | solution.py:13
  24.2 4.7 %collective-permute-start.3 = (bf16[36,384]{1,0:T(8,128)(2,1)S(1)}, bf16[36,384]{1,0:T(8,128)(2,1)S(1)}, u32[]{:S(2)}, u32[]{:S(2)}) collective-permute-start(bf16[36,384]{1,0:T(8,128)(2,1)S(1)} %get-tuple-element.29), channel_id=1, source_target_pairs={{0,1},{1,2},{2,3},{4,5},{5,6},{6,7},{8,9},{9,10},{10,11},{12,13},{... | collective-permute-start | bytes 82952 | tf_op jit(solution)/shard_map/ppermute | solution.py:13
  32.1 5.5 %collective-permute-start.4 = (f32[36,384]{1,0:T(8,128)S(1)}, f32[36,384]{1,0:T(8,128)S(1)}, u32[]{:S(2)}, u32[]{:S(2)}) collective-permute-start(f32[36,384]{1,0:T(8,128)S(1)} %slice.75), channel_id=1, source_target_pairs={{4,0},{8,4},{12,8},{16,12},{20,16},{24,20},{28,24},{32,28},{36,32}... | collective-permute-start | bytes 165896 | tf_op jit(solution)/shard_map/ppermute | solution.py:13
  37.7 5.3 %collective-permute-start.5 = (f32[36,384]{1,0:T(8,128)S(1)}, f32[36,384]{1,0:T(8,128)S(1)}, u32[]{:S(2)}, u32[]{:S(2)}) collective-permute-start(f32[36,384]{1,0:T(8,128)S(1)} %get-tuple-element.21), channel_id=1, source_target_pairs={{1,0},{2,1},{3,2},{5,4},{6,5},{7,6},{9,8},{10,9},{11,10},{13,12},{... | collective-permute-start | bytes 165896 | tf_op jit(solution)/shard_map/ppermute | solution.py:13
  263.8 5.0 %collective-permute-start.6 = (bf16[36,384]{1,0:T(8,128)(2,1)S(1)}, bf16[36,384]{1,0:T(8,128)(2,1)S(1)}, u32[]{:S(2)}, u32[]{:S(2)}) collective-permute-start(bf16[36,384]{1,0:T(8,128)(2,1)S(1)} %get-tuple-element.26), channel_id=1, source_target_pairs={{0,4},{4,8},{8,12},{12,16},{16,20},{20,24},{24,28},{28,32},{32,36}... | collective-permute-start | bytes 82952 | tf_op jit(solution)/shard_map/ppermute | solution.py:13
  265.7 4.1 %collective-permute-start.7 = (bf16[36,384]{1,0:T(8,128)(2,1)S(1)}, bf16[36,384]{1,0:T(8,128)(2,1)S(1)}, u32[]{:S(2)}, u32[]{:S(2)}) collective-permute-start(bf16[36,384]{1,0:T(8,128)(2,1)S(1)} %get-tuple-element.27), channel_id=1, source_target_pairs={{0,1},{1,2},{2,3},{4,5},{5,6},{6,7},{8,9},{9,10},{10,11},{12,13},{... | collective-permute-start | bytes 82952 | tf_op jit(solution)/shard_map/ppermute | solution.py:13
  273.0 5.5 %collective-permute-start.8 = (f32[36,384]{1,0:T(8,128)S(1)}, f32[36,384]{1,0:T(8,128)S(1)}, u32[]{:S(2)}, u32[]{:S(2)}) collective-permute-start(f32[36,384]{1,0:T(8,128)S(1)} %slice.81), channel_id=1, source_target_pairs={{4,0},{8,4},{12,8},{16,12},{20,16},{24,20},{28,24},{32,28},{36,32}... | collective-permute-start | bytes 165896 | tf_op jit(solution)/shard_map/ppermute | solution.py:13
  278.6 5.3 %collective-permute-start.9 = (f32[36,384]{1,0:T(8,128)S(1)}, f32[36,384]{1,0:T(8,128)S(1)}, u32[]{:S(2)}, u32[]{:S(2)}) collective-permute-start(f32[36,384]{1,0:T(8,128)S(1)} %get-tuple-element.20), channel_id=1, source_target_pairs={{1,0},{2,1},{3,2},{5,4},{6,5},{7,6},{9,8},{10,9},{11,10},{13,12},{... | collective-permute-start | bytes 165896 | tf_op jit(solution)/shard_map/ppermute | solution.py:13
where the time goes:
time: 398 us; the launch traced here: 397 us
  blocking collectives  332 us (83%)
  starting transfers between devices  33.4 us (8%)
  waiting for transfers between devices  14.8 us (4%)
  matrix products  9.69 us (2%)
    psum x3, blocking collectives, global_total(): return lax.psum(partial_value, ('sx', 'sy'))  332 us
    ppermute x10, starting transfers between devices, passed_along(): lax.ppermute(value, axis, [(source, source + steps) for source in range(i...  33.4 us
    ppermute x10, waiting for transfers between devices, passed_along(): lax.ppermute(value, axis, [(source, source + steps) for source in range(i...  14.8 us
    dot_general x3, matrix products, operate(): images = jnp.dot(pushed, flex_matrix, preferred_element_type=jnp.float32)  9.69 us
  transfers between devices with their start and end apart: 10, of which 7 were waited for; matrix products, arithmetic and copies ran while one was open for 1% of the time, Pallas kernels for 0%

commit v1 on v0

v1 whole, which is shorter than its diff:
```python
import functools

import jax
import jax.numpy as jnp
from jax import lax
from jax.experimental import pallas as pl
from jax.experimental.pallas import tpu as pltpu
from jax.sharding import PartitionSpec as P

FACE = 384
NB = 4 * FACE
HALF = 2 * FACE
LOADS = 36
NX, NY, NZ = 4, 8, 12
NSX = NZ * NY * 2
MESH = pl.DeviceIdType.MESH
F32 = jnp.float32
BF16 = jnp.bfloat16
ROWS = (1, 3, 0, 2)
COLS = (0, 2, 1, 3)


class Place:
    def __init__(self):
        self.sx = lax.axis_index("sx")
        self.sy = lax.axis_index("sy")
        self.core = lax.rem(self.sx, 2)
        self.y = lax.rem(self.sx // 2, NY)
        self.z = self.sx // (2 * NY)
        self.near = self.sy * 2 + self.core

    def down(self):
        return (lax.rem(self.sx + 1, NSX), self.sy)

    def up(self):
        return (lax.rem(self.sx + NSX - 1, NSX), self.sy)

    def right(self):
        return (self.sx, lax.rem(self.sy + 1, NX))

    def left(self):
        return (self.sx, lax.rem(self.sy + NX - 1, NX))

    def stage(self, which, k):
        if which == 0:
            slot = lax.rem(self.near + k, 2 * NX)
            return (self.sx - self.core + lax.rem(slot, 2), slot // 2)
        if which == 1:
            y = lax.rem(self.y + k, NY)
            return ((self.z * NY + y) * 2 + self.core, self.sy)
        z = lax.rem(self.z + k, NZ)
        return ((z * NY + self.y) * 2 + self.core, self.sy)

    def slot(self, which):
        return (self.near, self.y, self.z)[which]


STAGES = (2 * NX, NY, NZ)


def greet(place):
    barrier = pltpu.get_barrier_semaphore()
    peers = [place.down(), place.up()]
    for which, size in enumerate(STAGES):
        peers += [place.stage(which, k) for k in range(1, size)]
    for peer in peers:
        pl.semaphore_signal(barrier, inc=1, device_id=peer, device_id_type=MESH)
    return functools.partial(pl.semaphore_wait, barrier, len(peers))


def remote(src, dst, send_sem, recv_sem, peer):
    return pltpu.make_async_remote_copy(
        src_ref=src, dst_ref=dst, send_sem=send_sem, recv_sem=recv_sem, device_id=peer, device_id_type=MESH
    )


def diagonal(offset):
    row = lax.broadcasted_iota(jnp.int32, (LOADS, 128), 0)
    lane = lax.broadcasted_iota(jnp.int32, (LOADS, 128), 1)
    return lane == row + offset


def lanes(product, offset):
    column = jnp.sum(product, axis=1, keepdims=True)
    return jnp.sum(jnp.where(diagonal(offset), column, 0.0), axis=0, keepdims=True)


def column(row, offset):
    return jnp.sum(jnp.where(diagonal(offset), row, 0.0), axis=1, keepdims=True)


class Sums:
    def __init__(self, place, bufs, send_sems, recv_sems):
        self.place, self.bufs, self.send_sems, self.recv_sems = place, bufs, send_sems, recv_sems
        self.sent = []

    def __call__(self, index, value):
        for which, size in enumerate(STAGES):
            buf = self.bufs[which].at[index]
            mine = self.place.slot(which)
            buf[mine] = value
            copies = []
            for k in range(1, size):
                copies.append(
                    remote(
                        buf.at[mine],
                        buf.at[mine],
                        self.send_sems[which].at[index, k],
                        self.recv_sems[which].at[index, k],
                        self.place.stage(which, k),
                    )
                )
                copies[-1].start()
            for copy in copies:
                copy.wait_recv()
            value = buf[0]
            for k in range(1, size):
                value = value + buf[k]
            self.sent += copies
        return value


def exact_kernel(
    flex_hbm, loads_hbm, sizes_hbm, owner_hbm, out_ref,
    flex, loads, meta, z_out, z_in, u_out, u_in, acc, vec,
    buf0, buf1, buf2,
    load_sem, z_sem, u_sem, send0, send1, send2, recv0, recv1, recv2,
):
    place = Place()
    wait_all_in = greet(place)
    reads = start_reads(place, flex_hbm, loads_hbm, sizes_hbm, owner_hbm, flex, loads, meta, load_sem)
    total = Sums(place, (buf0, buf1, buf2), (send0, send1, send2), (recv0, recv1, recv2))
    sent = []

    for copy in reads["meta"] + reads["loads"]:
        copy.wait()
    cx, cy = coefficients(place, meta)

    def send_images(step):
        u_out[step, 0] = acc[:, 0:FACE]
        u_out[step, 1] = acc[:, FACE:HALF]
        copies = [
            remote(u_out.at[step, 0], u_in.at[step, 0], u_sem.at[0, step, 0], u_sem.at[1, step, 0], place.up()),
            remote(u_out.at[step, 1], u_in.at[step, 1], u_sem.at[0, step, 1], u_sem.at[1, step, 1], place.left()),
        ]
        for copy in copies:
            copy.start()
        sent.extend(copies)
        return copies

    def jumps(step, copies):
        for copy in copies:
            copy.wait_recv()
        jx = cx * (acc[:, HALF : HALF + FACE] - u_in[step, 0])
        jy = cy * (acc[:, HALF + FACE :] - u_in[step, 1])
        return jx, jy

    def operate(step, px, py):
        wx = (cx * px).astype(BF16)
        wy = (cy * py).astype(BF16)
        z_out[step, 0] = wx
        z_out[step, 1] = wy
        copies = [
            remote(z_out.at[step, 0], z_in.at[step, 0], z_sem.at[0, step, 0], z_sem.at[1, step, 0], place.down()),
            remote(z_out.at[step, 1], z_in.at[step, 1], z_sem.at[0, step, 1], z_sem.at[1, step, 1], place.right()),
        ]
        for copy in copies:
            copy.start()
        sent.extend(copies)
        own = jnp.concatenate([wx, wy], axis=1)
        acc[...] = jnp.dot(own, flex[0:HALF, :], preferred_element_type=F32)
        for copy in copies:
            copy.wait_recv()
        got = jnp.concatenate([-z_in[step, 0], -z_in[step, 1]], axis=1)
        acc[:, 0:HALF] += jnp.dot(got, flex[HALF:, 0:HALF], preferred_element_type=F32)
        copies = send_images(step + 1)
        acc[:, HALF:] += jnp.dot(got, flex[HALF:, HALF:], preferred_element_type=F32)
        return jumps(step + 1, copies)

    for copy in reads["low"]:
        copy.wait()
    acc[:, 0:HALF] = jnp.dot(loads[...], flex[:, 0:HALF], preferred_element_type=F32)
    wait_all_in()
    copies = send_images(0)
    for copy in reads["high"]:
        copy.wait()
    acc[:, HALF:] = jnp.dot(loads[...], flex[:, HALF:], preferred_element_type=F32)
    px, py = jumps(0, copies)
    vec[0, 0] = px
    vec[0, 1] = py
    qx, qy = operate(0, px, py)
    px, py = vec[0, 0], vec[0, 1]
    both = total(0, lanes(px * px + py * py, 0) + lanes(px * qx + py * qy, 64))
    rr = column(both, 0)
    step0 = rr / column(both, 64)
    rx = px - step0 * qx
    ry = py - step0 * qy
    vec[1, 0] = step0 * px
    vec[1, 1] = step0 * py
    s = column(total(1, lanes(rx * rx + ry * ry, 0)), 0)
    px = rx + (s / rr) * px
    py = ry + (s / rr) * py
    vec[0, 0] = px
    vec[0, 1] = py
    qx, qy = operate(1, px, py)
    px, py = vec[0, 0], vec[0, 1]
    step1 = s / column(total(2, lanes(px * qx + py * qy, 0)), 0)
    out_ref[0] = (vec[1, 0] + step1 * px).astype(BF16)
    out_ref[1] = (vec[1, 1] + step1 * py).astype(BF16)
    for copy in sent + total.sent:
        copy.wait_send()


def start_reads(place, flex_hbm, loads_hbm, sizes_hbm, owner_hbm, flex, loads, meta, sem):
    reads = {
        "meta": [
            pltpu.make_async_copy(sizes_hbm.at[place.sy], meta.at[0], sem.at[0]),
            pltpu.make_async_copy(owner_hbm.at[place.sy], meta.at[1], sem.at[1]),
        ],
        "loads": [],
        "low": [],
        "high": [],
    }
    count = 2
    for at, block in enumerate(ROWS):
        reads["loads"].append(
            pltpu.make_async_copy(
                loads_hbm.at[0, 0, :, pl.ds(block * FACE, FACE)], loads.at[:, pl.ds(at * FACE, FACE)], sem.at[count]
            )
        )
        count += 1
    for col_at, col in enumerate(COLS):
        for at, block in enumerate(ROWS):
            reads["low" if col_at < 2 else "high"].append(
                pltpu.make_async_copy(
                    flex_hbm.at[0, 0, pl.ds(block * FACE, FACE), pl.ds(col * FACE, FACE)],
                    flex.at[pl.ds(at * FACE, FACE), pl.ds(col_at * FACE, FACE)],
                    sem.at[count],
                )
            )
            count += 1
    for group in ("loads", "low", "meta", "high"):
        for copy in reads[group]:
            copy.start()
    return reads


def coefficients(place, meta):
    lane = lax.broadcasted_iota(jnp.int32, (2, NSX), 1)
    here = lane == place.sx
    sizes = jnp.sum(jnp.where(here, meta[0].astype(F32), 0.0), axis=1, keepdims=True)
    owner = jnp.sum(jnp.where(here, meta[1].astype(F32), 0.0), axis=1, keepdims=True)
    spot = lax.broadcasted_iota(jnp.int32, (1, FACE), 1).astype(F32)
    sign = 1.0 - 2.0 * owner
    has_x = jnp.where(place.sx < NSX - 1, 1.0, 0.0).astype(F32)
    has_y = jnp.where(place.sy < NX - 1, 1.0, 0.0).astype(F32)
    cx = jnp.where(spot < sizes[0:1] * has_x, sign[0:1], 0.0)
    cy = jnp.where(spot < sizes[1:2] * has_y, sign[1:2], 0.0)
    return cx, cy


READS = 2 + 4 + 16


def exact(flexibility, loads, sizes, owner):
    return pl.pallas_call(
        exact_kernel,
        out_shape=jax.ShapeDtypeStruct((2, LOADS, FACE), BF16),
        in_specs=[pl.BlockSpec(memory_space=pl.ANY)] * 4,
        out_specs=pl.BlockSpec(memory_space=pltpu.VMEM),
        scratch_shapes=[
            pltpu.VMEM((NB, NB), BF16),
            pltpu.VMEM((LOADS, NB), BF16),
            pltpu.VMEM((2, 2, NSX), jnp.int32),
            pltpu.VMEM((2, 2, LOADS, FACE), BF16),
            pltpu.VMEM((2, 2, LOADS, FACE), BF16),
            pltpu.VMEM((3, 2, LOADS, FACE), F32),
            pltpu.VMEM((3, 2, LOADS, FACE), F32),
            pltpu.VMEM((LOADS, NB), F32),
            pltpu.VMEM((2, 2, LOADS, FACE), F32),
        ]
        + [pltpu.VMEM((3, size, 1, 128), F32) for size in STAGES]
        + [
            pltpu.SemaphoreType.DMA((READS,)),
            pltpu.SemaphoreType.DMA((2, 2, 2)),
            pltpu.SemaphoreType.DMA((2, 3, 2)),
        ]
        + [pltpu.SemaphoreType.DMA((3, size)) for size in STAGES] * 2,
        compiler_params=pltpu.CompilerParams(collective_id=0, has_side_effects=True),
        name="exact",
    )(flexibility, loads, sizes, owner)


def body(flexibility, loads, face_sizes, face_owner):
    sizes = jnp.transpose(face_sizes, (1, 2, 0))
    owner = jnp.transpose(face_owner, (1, 2, 0))
    return exact(flexibility, loads, sizes, owner)[None, None]


def solution(mesh):
    return jax.shard_map(
        body,
        mesh=mesh,
        in_specs=(P("sx", "sy", None, None), P("sx", "sy", None, None), P(), P()),
        out_specs=P("sx", "sy", None, None, None),
        check_vma=False,
    )
```

time: 398 us -> 82.9 us (0.21)
  blocking collectives: 332 us -> 0 us
  Pallas kernels: 0 us -> 80.9 us
  starting transfers between devices: 33.4 us -> 0 us
  waiting for transfers between devices: 14.8 us -> 0 us
  matrix products: 9.69 us -> 0 us
    psum x3 -> x0, blocking collectives: 332 us -> none  [global_total(): return lax.psum(partial_value, ('sx', 'sy'))]
    pallas_call x0 -> x1, Pallas kernels: none -> 80.9 us  [exact(): pl.pallas_call(exact_kernel, out_shape=jax.ShapeDtypeStruct((2, LOADS, FA...]
    ppermute x10 -> x0, starting transfers between devices: 33.4 us -> none  [passed_along(): lax.ppermute(value, axis, [(source, source + steps) for source in range(i...]
    ppermute x10 -> x0, waiting for transfers between devices: 14.8 us -> none  [passed_along(): lax.ppermute(value, axis, [(source, source + steps) for source in range(i...]
    dot_general x3 -> x0, matrix products: 9.69 us -> none  [operate(): images = jnp.dot(pushed, flex_matrix, preferred_element_type=jnp.float32)]
  transfers between devices with their start and end apart: 10 -> 0, of which waited for: 7 -> 0; matrix products, arithmetic and copies ran while one was open for 1% -> 0% of each run, Pallas kernels for 0% -> 0%
where the time goes in v1:
time: 82.9 us; the launch traced here: 82.4 us
  Pallas kernels  80.9 us (98%)
  local copies, waits for them, and re-layouts  1.49 us (2%)
    pallas_call x1, Pallas kernels, exact(): pl.pallas_call(exact_kernel, out_shape=jax.ShapeDtypeStruct((2, LOADS, FA...  80.9 us

profile of v1, /device:TPU:1, one launch (start us, length us, event | category | flops | bytes accessed | tf_op | source)
XLA Modules:
  0.0 82.4 jit_solution(7466052308619461559)
XLA Ops:
  0.0 80.9 %exact.1 = bf16[2,36,384]{2,1,0:T(8,128)(2,1)} custom-call(bf16[1,1,1536,1536]{3,2,1,0:T(8,128)(2,1)} %flex_hbm.1, bf16[1,1,36,1536]{3,2,1,0:T(8,128)(2,1)} %loads_hbm.1, s32[4,2,192]{2,1,0:T(2,128)} %bitcast.4, s32[4,2,192]{2,1,0:T(2,128)} %bitcast.5), custom_call_target="tpu_custom_call" | custom-call | tf_op jit(solution)/shard_map/exact/pallas_call | solution.py:266
  80.9 1.5 %copy.5 = bf16[1,1,2,36,384]{4,2,3,1,0:T(2,128)(2,1)} copy(bf16[1,1,2,36,384]{4,3,2,1,0:T(8,128)(2,1)} %bitcast.3) | data formatting | bytes 110592 | tf_op jit(solution)/shard_map/broadcast_in_dim | solution.py:297

commit v2 on v1

--- a/solution.py
+++ b/solution.py
@@ -291,11 +291,152 @@
     )(flexibility, loads, sizes, owner)
 
 
+def fast_kernel(
+    flex_hbm, loads_hbm, sizes_hbm, owner_hbm, out_ref, good_ref,
+    flex, loads, meta, z_out, z_in, d_out, d_in, q_out, q_in, acc, vec,
+    buf0, buf1, buf2,
+    load_sem, z_sem, u_sem, send0, send1, send2, recv0, recv1, recv2,
+):
+    place = Place()
+    wait_all_in = greet(place)
+    reads = start_reads(place, flex_hbm, loads_hbm, sizes_hbm, owner_hbm, flex, loads, meta, load_sem)
+    total = Sums(place, (buf0, buf1, buf2), (send0, send1, send2), (recv0, recv1, recv2))
+    sent = []
+
+    for copy in reads["meta"] + reads["loads"]:
+        copy.wait()
+    cx, cy = coefficients(place, meta)
+
+    def send_images(step, out, into):
+        out[0] = acc[:, 0:FACE].astype(out.dtype)
+        out[1] = acc[:, FACE:HALF].astype(out.dtype)
+        copies = [
+            remote(out.at[0], into.at[0], u_sem.at[0, step, 0], u_sem.at[1, step, 0], place.up()),
+            remote(out.at[1], into.at[1], u_sem.at[0, step, 1], u_sem.at[1, step, 1], place.left()),
+        ]
+        for copy in copies:
+            copy.start()
+        sent.extend(copies)
+        return copies
+
+    def jumps(copies, into):
+        for copy in copies:
+            copy.wait_recv()
+        jx = cx * (acc[:, HALF : HALF + FACE] - into[0].astype(F32))
+        jy = cy * (acc[:, HALF + FACE :] - into[1].astype(F32))
+        return jx, jy
+
+    def send_search(step, vx, vy):
+        wx = (cx * vx).astype(BF16)
+        wy = (cy * vy).astype(BF16)
+        z_out[step, 0] = wx
+        z_out[step, 1] = wy
+        copies = [
+            remote(z_out.at[step, 0], z_in.at[step, 0], z_sem.at[0, step, 0], z_sem.at[1, step, 0], place.down()),
+            remote(z_out.at[step, 1], z_in.at[step, 1], z_sem.at[0, step, 1], z_sem.at[1, step, 1], place.right()),
+        ]
+        for copy in copies:
+            copy.start()
+        sent.extend(copies)
+        own = jnp.concatenate([wx, wy], axis=1)
+        acc[...] = jnp.dot(own, flex[0:HALF, :], preferred_element_type=F32)
+        return own, copies
+
+    for copy in reads["low"]:
+        copy.wait()
+    acc[:, 0:HALF] = jnp.dot(loads[...], flex[:, 0:HALF], preferred_element_type=F32)
+    wait_all_in()
+    copies = send_images(0, d_out, d_in)
+    for copy in reads["high"]:
+        copy.wait()
+    acc[:, HALF:] = jnp.dot(loads[...], flex[:, HALF:], preferred_element_type=F32)
+    dx, dy = jumps(copies, d_in)
+    own, copies = send_search(0, dx, dy)
+    vec[0, 0] = dx
+    vec[0, 1] = dy
+    for copy in copies:
+        copy.wait_recv()
+    got = jnp.concatenate([-z_in[0, 0], -z_in[0, 1]], axis=1)
+    acc[:, 0:HALF] += jnp.dot(got, flex[HALF:, 0:HALF], preferred_element_type=F32)
+    copies = send_images(1, q_out, q_in)
+    acc[:, HALF:] += jnp.dot(got, flex[HALF:, HALF:], preferred_element_type=F32)
+    qx, qy = jumps(copies, q_in)
+    own, copies = send_search(1, qx, qy)
+    vec[1, 0] = qx
+    vec[1, 1] = qy
+    dx, dy = vec[0, 0], vec[0, 1]
+    top = lanes(dx * dx + dy * dy, 0) + lanes(dx * qx + dy * qy, 64)
+    bottom = lanes(qx * qx + qy * qy, 0)
+    kept = own.astype(F32) * acc[:, HALF:]
+    for copy in copies:
+        copy.wait_recv()
+    got = jnp.concatenate([z_in[1, 0], z_in[1, 1]], axis=1)
+    crossed = jnp.dot(got, flex[HALF:, 0:HALF], preferred_element_type=F32) - 2.0 * acc[:, 0:HALF]
+    bottom = bottom + lanes(kept + got.astype(F32) * crossed, 64)
+    sums = total(0, jnp.concatenate([top, bottom], axis=0))
+    dd, dq = column(sums[0:1], 0), column(sums[0:1], 64)
+    qq, qw = column(sums[1:2], 0), column(sums[1:2], 64)
+    a = dd / dq
+    far = a * a * qq
+    s = far - dd
+    g = far / dd
+    weight = a * a * qw
+    curve = g * g * dq - 2.0 * a * g * qq + weight
+    a1 = s / curve
+    alpha = a + a1 * g
+    beta = -a1 * a
+    out_ref[0] = (alpha * vec[0, 0] + beta * vec[1, 0]).astype(BF16)
+    out_ref[1] = (alpha * vec[0, 1] + beta * vec[1, 1]).astype(BF16)
+    good = (s >= CLOSE * dd) & (curve >= CLOSE * weight) & (s < TOP) & (curve < TOP)
+    for value in (dd, dq, qq, qw):
+        good = good & (value > 1.0 / TOP) & (value < TOP)
+    good_ref[0] = jnp.min(jnp.where(good, 1.0, 0.0)).astype(jnp.int32)
+    for copy in sent + total.sent:
+        copy.wait_send()
+
+
+CLOSE = 2.0**-6
+TOP = 1e30
+
+
+def fast(flexibility, loads, sizes, owner):
+    return pl.pallas_call(
+        fast_kernel,
+        out_shape=(jax.ShapeDtypeStruct((2, LOADS, FACE), BF16), jax.ShapeDtypeStruct((1,), jnp.int32)),
+        in_specs=[pl.BlockSpec(memory_space=pl.ANY)] * 4,
+        out_specs=(pl.BlockSpec(memory_space=pltpu.VMEM), pl.BlockSpec(memory_space=pltpu.SMEM)),
+        scratch_shapes=[
+            pltpu.VMEM((NB, NB), BF16),
+            pltpu.VMEM((LOADS, NB), BF16),
+            pltpu.VMEM((2, 2, NSX), jnp.int32),
+            pltpu.VMEM((2, 2, LOADS, FACE), BF16),
+            pltpu.VMEM((2, 2, LOADS, FACE), BF16),
+            pltpu.VMEM((2, LOADS, FACE), F32),
+            pltpu.VMEM((2, LOADS, FACE), F32),
+            pltpu.VMEM((2, LOADS, FACE), BF16),
+            pltpu.VMEM((2, LOADS, FACE), BF16),
+            pltpu.VMEM((LOADS, NB), F32),
+            pltpu.VMEM((2, 2, LOADS, FACE), F32),
+        ]
+        + [pltpu.VMEM((1, size, 2, 128), F32) for size in STAGES]
+        + [
+            pltpu.SemaphoreType.DMA((READS,)),
+            pltpu.SemaphoreType.DMA((2, 2, 2)),
+            pltpu.SemaphoreType.DMA((2, 2, 2)),
+        ]
+        + [pltpu.SemaphoreType.DMA((1, size)) for size in STAGES] * 2,
+        compiler_params=pltpu.CompilerParams(collective_id=1, has_side_effects=True),
+        name="fast",
+    )(flexibility, loads, sizes, owner)
+
+
 def body(flexibility, loads, face_sizes, face_owner):
     sizes = jnp.transpose(face_sizes, (1, 2, 0))
     owner = jnp.transpose(face_owner, (1, 2, 0))
-    return exact(flexibility, loads, sizes, owner)[None, None]
-
+    args = (flexibility, loads, sizes, owner)
+    result, good = fast(*args)
+    result = lax.cond(good[0] > 0, lambda: result, lambda: exact(*args))
+    return result[None, None]
 
 def solution(mesh):
     return jax.shard_map(

time: 82.9 us -> 49.7 us (0.60)
  Pallas kernels: 80.9 us -> 48.2 us
    pallas_call x1, Pallas kernels: 80.9 us -> 48.2 us  [fast(): pl.pallas_call(fast_kernel, out_shape=(jax.ShapeDtypeStruct((2, LOADS, FA...]
    broadcast_in_dim x1 -> x0, local copies, waits for them, and re-layouts: 1.49 us -> none  [body(): return exact(flexibility, loads, sizes, owner)[None, None]]
where the time goes in v2:
time: 49.7 us; the launch traced here: 49.6 us
  Pallas kernels  48.2 us (97%)
  between operations  0.74 us (1%)
  local copies, waits for them, and re-layouts  0.67 us (1%)
    pallas_call x1, Pallas kernels, fast(): pl.pallas_call(fast_kernel, out_shape=(jax.ShapeDtypeStruct((2, LOADS, FA...  48.2 us

profile of v2, /device:TPU:1, one launch (start us, length us, event | category | flops | bytes accessed | tf_op | source)
XLA Modules:
  0.0 49.6 jit_solution(1689644465105829065)
XLA Ops:
  0.0 0.0 copy-start
  0.0 0.0 copy-start.3
  0.0 0.0 copy-start.2
  0.0 48.2 %fast.1 = (bf16[2,36,384]{2,1,0:T(8,128)(2,1)S(1)}, s32[1]{0:T(128)}) custom-call(bf16[1,1,1536,1536]{3,2,1,0:T(8,128)(2,1)} %flex_hbm.1, bf16[1,1,36,1536]{3,2,1,0:T(8,128)(2,1)} %loads_hbm.1, s32[4,2,192]{2,1,0:T(2,128)} %bitcast.7, s32[4,2,192]{2,1,0:T(2,128)} %bitcast.9), custom_call_target="tpu_custom_call" | custom-call | tf_op jit(solution)/shard_map/fast/pallas_call | solution.py:403
  48.9 0.0 copy-done
  48.9 0.0 copy-done.3
  48.9 0.0 copy-done.2
  48.9 0.1 conditional.1
  49.0 0.0 copy-start.1
  49.0 0.6 %copy-done.1 = bf16[1,1,2,36,384]{4,2,3,1,0:T(2,128)(2,1)} copy-done((bf16[1,1,2,36,384]{4,2,3,1,0:T(2,128)(2,1)}, bf16[1,1,2,36,384]{4,2,3,1,0:T(2,128)(2,1)S(1)}, u32[]{:S(2)}) %copy-start.1) | copy-done | bytes 55320
  (1 shorter events, 0.0 us)
Async XLA Ops:
  0.0 48.9 %copy-start = (bf16[1,1,36,1536]{3,2,1,0:T(8,128)(2,1)S(1)}, bf16[1,1,36,1536]{3,2,1,0:T(8,128)(2,1)}, u32[]{:S(2)}) copy-start(bf16[1,1,36,1536]{3,2,1,0:T(8,128)(2,1)} %loads_hbm.1) | copy-start | bytes 331780
  0.0 48.9 %copy-start.3 = (s32[192,4,2]{0,2,1:T(2,128)S(1)}, s32[192,4,2]{0,2,1:T(2,128)}, u32[]{:S(2)}) copy-start(s32[192,4,2]{0,2,1:T(2,128)} %param.9) | copy-start | bytes 18436
  0.0 48.9 %copy-start.2 = (s32[192,4,2]{0,2,1:T(2,128)S(1)}, s32[192,4,2]{0,2,1:T(2,128)}, u32[]{:S(2)}) copy-start(s32[192,4,2]{0,2,1:T(2,128)} %param.8) | copy-start | bytes 18436
  49.0 0.6 %copy-start.1 = (bf16[1,1,2,36,384]{4,2,3,1,0:T(2,128)(2,1)}, bf16[1,1,2,36,384]{4,2,3,1,0:T(2,128)(2,1)S(1)}, u32[]{:S(2)}) copy-start(bf16[1,1,2,36,384]{4,2,3,1,0:T(2,128)(2,1)S(1)} %get-tuple-element.31) | copy-start | bytes 165892

commit v3 on v1

--- a/solution.py
+++ b/solution.py
@@ -291,11 +291,268 @@
     )(flexibility, loads, sizes, owner)
 
 
+def far(size, k):
+    return min(k, size - k)
+
+
+PLANE = sorted(((x, y) for x in range(NX) for y in range(NY) if x or y), key=lambda o: -far(NX, o[0]) - far(NY, o[1]))
+LINE = sorted(((z, c) for z in range(NZ) for c in range(2) if z or c), key=lambda o: -2 * far(NZ, o[0]) - o[1])
+
+
+class Partners:
+    def __init__(self, place):
+        self.slots = (place.sy * NY + place.y, place.z * 2 + place.core)
+        plane = [
+            ((place.z * NY + lax.rem(place.y + y, NY)) * 2 + place.core, lax.rem(place.sy + x, NX)) for x, y in PLANE
+        ]
+        line = [
+            (
+                (lax.rem(place.z + z, NZ) * NY + place.y) * 2 + (1 - place.core if c else place.core),
+                place.sy,
+            )
+            for z, c in LINE
+        ]
+        self.stages = (plane, line)
+        self.core = (place.sx + 1 - 2 * place.core, place.sy)
+
+    @staticmethod
+    def along_y(place, k):
+        return ((place.z * NY + lax.rem(place.y + k + NY, NY)) * 2 + place.core, place.sy)
+
+    @staticmethod
+    def along_z(place, k):
+        return ((lax.rem(place.z + k + NZ, NZ) * NY + place.y) * 2 + place.core, place.sy)
+
+
+def fast_kernel(
+    flex_hbm, loads_hbm, sizes_hbm, owner_hbm, out_ref, good_ref,
+    flex, loads, meta, sign_meta, u0, r0, u1, r1, dvec, qvec,
+    buf0, buf1,
+    load_sem, u_sem, sum_sem, word,
+):
+    place = Place()
+    left_sy = lax.rem(place.sy + NX - 1, NX)
+    sem = iter(range(FAST_READS))
+    load_read = pltpu.make_async_copy(loads_hbm.at[0, 0], loads, load_sem.at[next(sem)])
+    flex_reads = {}
+    for half in (1, 0):
+        for block in range(4):
+            spot = (pl.ds(block * FACE, FACE), pl.ds(half * HALF, HALF))
+            flex_reads[half, block] = pltpu.make_async_copy(
+                flex_hbm.at[(0, 0) + spot], flex.at[spot], load_sem.at[next(sem)]
+            )
+    meta_reads = [
+        pltpu.make_async_copy(sizes_hbm.at[place.sy], meta.at[0], load_sem.at[next(sem)]),
+        pltpu.make_async_copy(sizes_hbm.at[left_sy], meta.at[1], load_sem.at[next(sem)]),
+        pltpu.make_async_copy(owner_hbm.at[place.sy], sign_meta, load_sem.at[next(sem)]),
+    ]
+    load_read.start()
+    for half in (1, 0):
+        for block in range(4):
+            flex_reads[half, block].start()
+    for copy in meta_reads:
+        copy.start()
+    partners = Partners(place)
+    faces = (place.up(), place.down(), place.left(), place.right())
+    near_y, near_z = [[along(place, k) for k in (1, -1)] for along in (partners.along_y, partners.along_z)]
+    next_y, next_z = [[along(place, k) for k in (2, -2)] for along in (partners.along_y, partners.along_z)]
+    rounds = (
+        near_y + near_z,
+        next_y + next_z,
+        next_z + list(faces[2:]),
+        [partners.core] + list(faces[2:]),
+    )
+    barrier = pltpu.get_barrier_semaphore()
+    peers = list(faces) + near_y + near_z
+    for peer in peers:
+        pl.semaphore_signal(barrier, inc=1, device_id=peer, device_id_type=MESH)
+
+    def tell(which):
+        for peer in rounds[which]:
+            pl.semaphore_signal(word.at[which], inc=1, device_id=peer, device_id_type=MESH)
+
+    def hear(which):
+        pl.semaphore_wait(word.at[which], len(rounds[which]))
+
+    sent = []
+
+    def exchange(step, half, source, into):
+        copies = []
+        for block in (2 * half, 2 * half + 1):
+            copies.append(
+                remote(
+                    source.at[block], into.at[block ^ 1], u_sem.at[0, step, block], u_sem.at[1, step, block], faces[block]
+                )
+            )
+            copies[-1].start()
+        sent.extend(copies)
+        return copies
+
+    def product(rows, half, block):
+        return jnp.dot(
+            rows, flex[block * FACE : (block + 1) * FACE, half * HALF : (half + 1) * HALF], preferred_element_type=F32
+        )
+
+    def half_product(pair, row_half, col_half):
+        return jnp.dot(
+            pair,
+            flex[row_half * HALF : (row_half + 1) * HALF, col_half * HALF : (col_half + 1) * HALF],
+            preferred_element_type=F32,
+        )
+
+    load_read.wait()
+    copies0 = {}
+    for half in (1, 0):
+        for block in range(2):
+            flex_reads[half, block].wait()
+        value = half_product(loads[:, 0:HALF], 0, half)
+        for block in range(2, 4):
+            flex_reads[half, block].wait()
+        value = value + half_product(loads[:, HALF:], 1, half)
+        u0[2 * half] = value[:, 0:FACE]
+        u0[2 * half + 1] = value[:, FACE:]
+        if half == 1:
+            pl.semaphore_wait(barrier, len(peers))
+        copies0[half] = exchange(0, half, u0, r0)
+        if half == 1:
+            tell(0)
+    for copy in meta_reads:
+        copy.wait()
+    hear(0)
+    tell(1)
+    live, sign = live_faces(place, meta, sign_meta)
+    hear(1)
+    tell(2)
+
+    def jump(half, copies, u, r, kept):
+        for copy in copies[half]:
+            copy.wait_recv()
+        pair = []
+        for block in (2 * half, 2 * half + 1):
+            value = jnp.where(live[block], u[block] - r[block], 0.0)
+            kept[block] = value
+            pair.append(value.astype(BF16))
+        return jnp.concatenate(pair, axis=1)
+
+    pair = jump(0, copies0, u0, r0, dvec)
+    low = [half_product(pair, 0, half) for half in range(2)]
+    pair = jump(1, copies0, u0, r0, dvec)
+    copies1 = {}
+    for half in (1, 0):
+        value = low[half] + half_product(pair, 1, half)
+        u1[2 * half] = value[:, 0:FACE]
+        u1[2 * half + 1] = value[:, FACE:]
+        copies1[half] = exchange(1, half, u1, r1)
+    hear(2)
+    tell(3)
+    top = lanes(dvec[1] * dvec[1] + dvec[3] * dvec[3], 0)
+    first = jump(0, copies1, u1, r1, qvec)
+    low = [half_product(first, 0, half) for half in range(2)]
+    second = jump(1, copies1, u1, r1, qvec)
+    inner = first.astype(F32) * low[0]
+    inner = inner + second.astype(F32) * (2.0 * low[1] + half_product(second, 1, 1))
+    top = top + lanes(dvec[1] * qvec[1] + dvec[3] * qvec[3], 64)
+    bottom = lanes(qvec[1] * qvec[1] + qvec[3] * qvec[3], 0) + lanes(inner, 64)
+    sums = jnp.concatenate([top, bottom], axis=0)
+    hear(3)
+    waits = []
+    for which, (stage, mine, buf) in enumerate(zip(partners.stages, partners.slots, (buf0, buf1))):
+        buf[mine] = sums
+        for peer in stage:
+            remote(buf.at[mine], buf.at[mine], sum_sem.at[0, which], sum_sem.at[1, which], peer).start()
+        others = buf.at[pl.ds(0, len(stage))]
+        waits.append(remote(others, others, sum_sem.at[0, which], sum_sem.at[1, which], stage[0]))
+        waits[-1].wait_recv()
+        terms = [buf[k] for k in range(len(stage) + 1)]
+        while len(terms) > 1:
+            terms = [sum(terms[k : k + 2]) for k in range(0, len(terms), 2)]
+        sums = terms[0]
+    dd, dq = column(sums[0:1], 0), column(sums[0:1], 64)
+    qq, qw = column(sums[1:2], 0), column(sums[1:2], 64)
+    a = dd / dq
+    far = a * a * qq
+    s = far - dd
+    g = far / dd
+    weight = a * a * qw
+    curve = g * g * dq - 2.0 * a * g * qq + weight
+    a1 = s / curve
+    alpha = a + a1 * g
+    beta = -a1 * a
+    out_ref[0] = (sign[0] * (alpha * dvec[1] + beta * qvec[1])).astype(BF16)
+    out_ref[1] = (sign[1] * (alpha * dvec[3] + beta * qvec[3])).astype(BF16)
+    good = (s >= CLOSE * dd) & (curve >= CLOSE * weight) & (s < TOP) & (curve < TOP)
+    for value in (dd, dq, qq, qw):
+        good = good & (value > 1.0 / TOP) & (value < TOP)
+    good_ref[0] = jnp.min(jnp.where(good, 1.0, 0.0)).astype(jnp.int32)
+    for copy in sent + waits:
+        copy.wait_send()
+
+
+def live_faces(place, meta, sign_meta):
+    lane = lax.broadcasted_iota(jnp.int32, (2, NSX), 1)
+
+    def at(table, row):
+        return jnp.sum(jnp.where(lane == row, table.astype(F32), 0.0), axis=1, keepdims=True)
+
+    here = at(meta[0], place.sx)
+    sizes = (
+        at(meta[0], place.sx - 1)[0:1],
+        here[0:1] * jnp.where(place.sx < NSX - 1, 1.0, 0.0).astype(F32),
+        at(meta[1], place.sx)[1:2] * jnp.where(place.sy > 0, 1.0, 0.0).astype(F32),
+        here[1:2] * jnp.where(place.sy < NX - 1, 1.0, 0.0).astype(F32),
+    )
+    spot = lax.broadcasted_iota(jnp.int32, (LOADS, FACE), 1).astype(F32)
+    sign = 1.0 - 2.0 * at(sign_meta[...], place.sx)
+    return [spot < size for size in sizes], (sign[0:1], sign[1:2])
+
+
+FAST_READS = 1 + 8 + 3
+
+
+CLOSE = 2.0**-6
+TOP = 1e30
+
+
+def fast(flexibility, loads, sizes, owner):
+    def faces(dtype):
+        return pltpu.VMEM((4, LOADS, FACE), dtype)
+
+    return pl.pallas_call(
+        fast_kernel,
+        out_shape=(jax.ShapeDtypeStruct((2, LOADS, FACE), BF16), jax.ShapeDtypeStruct((1,), jnp.int32)),
+        in_specs=[pl.BlockSpec(memory_space=pl.ANY)] * 4,
+        out_specs=(pl.BlockSpec(memory_space=pltpu.VMEM), pl.BlockSpec(memory_space=pltpu.SMEM)),
+        scratch_shapes=[
+            pltpu.VMEM((NB, NB), BF16),
+            pltpu.VMEM((LOADS, NB), BF16),
+            pltpu.VMEM((2, 2, NSX), jnp.int32),
+            pltpu.VMEM((2, NSX), jnp.int32),
+            faces(F32),
+            faces(F32),
+            faces(F32),
+            faces(F32),
+            faces(F32),
+            faces(F32),
+        ]
+        + [pltpu.VMEM((size, 2, 128), F32) for size in (NX * NY, 2 * NZ)]
+        + [
+            pltpu.SemaphoreType.DMA((FAST_READS,)),
+            pltpu.SemaphoreType.DMA((2, 2, 4)),
+            pltpu.SemaphoreType.DMA((2, 2)),
+            pltpu.SemaphoreType.REGULAR((4,)),
+        ],
+        compiler_params=pltpu.CompilerParams(collective_id=1, has_side_effects=True),
+        name="fast",
+    )(flexibility, loads, sizes, owner)
+
+
 def body(flexibility, loads, face_sizes, face_owner):
     sizes = jnp.transpose(face_sizes, (1, 2, 0))
     owner = jnp.transpose(face_owner, (1, 2, 0))
-    return exact(flexibility, loads, sizes, owner)[None, None]
-
+    args = (flexibility, loads, sizes, owner)
+    result, good = fast(*args)
+    result = lax.cond(good[0] > 0, lambda: result, lambda: exact(*args))
+    return result[None, None]
 
 def solution(mesh):
     return jax.shard_map(

time: 82.9 us -> 41.5 us (0.50)
  Pallas kernels: 80.9 us -> 39.9 us
    pallas_call x1, Pallas kernels: 80.9 us -> 39.9 us  [fast(): pl.pallas_call(fast_kernel, out_shape=(jax.ShapeDtypeStruct((2, LOADS, FA...]
    broadcast_in_dim x1 -> x0, local copies, waits for them, and re-layouts: 1.49 us -> none  [body(): return exact(flexibility, loads, sizes, owner)[None, None]]
where the time goes in v3:
time: 41.5 us; the launch traced here: 41.4 us
  Pallas kernels  39.9 us (96%)
  between operations  0.74 us (2%)
  local copies, waits for them, and re-layouts  0.67 us (2%)
    pallas_call x1, Pallas kernels, fast(): pl.pallas_call(fast_kernel, out_shape=(jax.ShapeDtypeStruct((2, LOADS, FA...  39.9 us

profile of v3, /device:TPU:1, one launch (start us, length us, event | category | flops | bytes accessed | tf_op | source)
XLA Modules:
  0.0 41.4 jit_solution(14555796829268621125)
XLA Ops:
  0.0 0.0 copy-start
  0.0 0.0 copy-start.3
  0.0 0.0 copy-start.2
  0.0 39.9 %fast.1 = (bf16[2,36,384]{2,1,0:T(8,128)(2,1)S(1)}, s32[1]{0:T(128)}) custom-call(bf16[1,1,1536,1536]{3,2,1,0:T(8,128)(2,1)} %flex_hbm.1, bf16[1,1,36,1536]{3,2,1,0:T(8,128)(2,1)} %loads_hbm.1, s32[4,2,192]{2,1,0:T(2,128)} %bitcast.7, s32[4,2,192]{2,1,0:T(2,128)} %bitcast.9), custom_call_target="tpu_custom_call" | custom-call | tf_op jit(solution)/shard_map/fast/pallas_call | solution.py:520
  40.6 0.0 copy-done
  40.7 0.0 copy-done.3
  40.7 0.0 copy-done.2
  40.7 0.1 conditional.1
  40.7 0.0 copy-start.1
  40.8 0.6 %copy-done.1 = bf16[1,1,2,36,384]{4,2,3,1,0:T(2,128)(2,1)} copy-done((bf16[1,1,2,36,384]{4,2,3,1,0:T(2,128)(2,1)}, bf16[1,1,2,36,384]{4,2,3,1,0:T(2,128)(2,1)S(1)}, u32[]{:S(2)}) %copy-start.1) | copy-done | bytes 55320
  (1 shorter events, 0.0 us)
Async XLA Ops:
  0.0 40.6 %copy-start = (bf16[1,1,36,1536]{3,2,1,0:T(8,128)(2,1)S(1)}, bf16[1,1,36,1536]{3,2,1,0:T(8,128)(2,1)}, u32[]{:S(2)}) copy-start(bf16[1,1,36,1536]{3,2,1,0:T(8,128)(2,1)} %loads_hbm.1) | copy-start | bytes 331780
  0.0 40.7 %copy-start.3 = (s32[192,4,2]{0,2,1:T(2,128)S(1)}, s32[192,4,2]{0,2,1:T(2,128)}, u32[]{:S(2)}) copy-start(s32[192,4,2]{0,2,1:T(2,128)} %param.9) | copy-start | bytes 18436
  0.0 40.7 %copy-start.2 = (s32[192,4,2]{0,2,1:T(2,128)S(1)}, s32[192,4,2]{0,2,1:T(2,128)}, u32[]{:S(2)}) copy-start(s32[192,4,2]{0,2,1:T(2,128)} %param.8) | copy-start | bytes 18436
  40.7 0.6 %copy-start.1 = (bf16[1,1,2,36,384]{4,2,3,1,0:T(2,128)(2,1)}, bf16[1,1,2,36,384]{4,2,3,1,0:T(2,128)(2,1)S(1)}, u32[]{:S(2)}) copy-start(bf16[1,1,2,36,384]{4,2,3,1,0:T(2,128)(2,1)S(1)} %get-tuple-element.31) | copy-start | bytes 165892

commit v4 on v3

--- a/solution.py
+++ b/solution.py
@@ -205,8 +205,7 @@
     qx, qy = operate(1, px, py)
     px, py = vec[0, 0], vec[0, 1]
     step1 = s / column(total(2, lanes(px * qx + py * qy, 0)), 0)
-    out_ref[0] = (vec[1, 0] + step1 * px).astype(BF16)
-    out_ref[1] = (vec[1, 1] + step1 * py).astype(BF16)
+    out_ref[...] = jnp.stack([vec[1, 0] + step1 * px, vec[1, 1] + step1 * py], axis=1).astype(BF16)
     for copy in sent + total.sent:
         copy.wait_send()
 
@@ -265,7 +264,7 @@
 def exact(flexibility, loads, sizes, owner):
     return pl.pallas_call(
         exact_kernel,
-        out_shape=jax.ShapeDtypeStruct((2, LOADS, FACE), BF16),
+        out_shape=jax.ShapeDtypeStruct((LOADS, 2, FACE), BF16),
         in_specs=[pl.BlockSpec(memory_space=pl.ANY)] * 4,
         out_specs=pl.BlockSpec(memory_space=pltpu.VMEM),
         scratch_shapes=[
@@ -326,7 +325,7 @@
 
 def fast_kernel(
     flex_hbm, loads_hbm, sizes_hbm, owner_hbm, out_ref, good_ref,
-    flex, loads, meta, sign_meta, u0, r0, u1, r1, dvec, qvec,
+    flex, loads, meta, sign_meta, u0, r0, u1, r1, dvec, qvec, low_ref,
     buf0, buf1,
     load_sem, u_sem, sum_sem, word,
 ):
@@ -403,12 +402,19 @@
     load_read.wait()
     copies0 = {}
     for half in (1, 0):
+        if half == 0:
+            low_ref[0] = lax.dot_general(
+                loads[:, HALF:], flex[0:HALF, HALF:], (((1,), (1,)), ((), ())), preferred_element_type=F32
+            )
         for block in range(2):
             flex_reads[half, block].wait()
         value = half_product(loads[:, 0:HALF], 0, half)
-        for block in range(2, 4):
-            flex_reads[half, block].wait()
-        value = value + half_product(loads[:, HALF:], 1, half)
+        if half == 1:
+            for block in range(2, 4):
+                flex_reads[half, block].wait()
+            value = value + half_product(loads[:, HALF:], 1, half)
+        else:
+            value = value + low_ref[0]
         u0[2 * half] = value[:, 0:FACE]
         u0[2 * half + 1] = value[:, FACE:]
         if half == 1:
@@ -435,11 +441,14 @@
         return jnp.concatenate(pair, axis=1)
 
     pair = jump(0, copies0, u0, r0, dvec)
-    low = [half_product(pair, 0, half) for half in range(2)]
+    for half in range(2):
+        low_ref[half] = half_product(pair, 0, half)
+    for block in range(2, 4):
+        flex_reads[0, block].wait()
     pair = jump(1, copies0, u0, r0, dvec)
     copies1 = {}
     for half in (1, 0):
-        value = low[half] + half_product(pair, 1, half)
+        value = low_ref[half] + half_product(pair, 1, half)
         u1[2 * half] = value[:, 0:FACE]
         u1[2 * half + 1] = value[:, FACE:]
         copies1[half] = exchange(1, half, u1, r1)
@@ -447,10 +456,11 @@
     tell(3)
     top = lanes(dvec[1] * dvec[1] + dvec[3] * dvec[3], 0)
     first = jump(0, copies1, u1, r1, qvec)
-    low = [half_product(first, 0, half) for half in range(2)]
+    inner = first.astype(F32) * half_product(first, 0, 0)
+    low_ref[0] = inner
+    low_ref[1] = 2.0 * half_product(first, 0, 1)
     second = jump(1, copies1, u1, r1, qvec)
-    inner = first.astype(F32) * low[0]
-    inner = inner + second.astype(F32) * (2.0 * low[1] + half_product(second, 1, 1))
+    inner = low_ref[0] + second.astype(F32) * (low_ref[1] + half_product(second, 1, 1))
     top = top + lanes(dvec[1] * qvec[1] + dvec[3] * qvec[3], 64)
     bottom = lanes(qvec[1] * qvec[1] + qvec[3] * qvec[3], 0) + lanes(inner, 64)
     sums = jnp.concatenate([top, bottom], axis=0)
@@ -478,8 +488,9 @@
     a1 = s / curve
     alpha = a + a1 * g
     beta = -a1 * a
-    out_ref[0] = (sign[0] * (alpha * dvec[1] + beta * qvec[1])).astype(BF16)
-    out_ref[1] = (sign[1] * (alpha * dvec[3] + beta * qvec[3])).astype(BF16)
+    mx = sign[0] * (alpha * dvec[1] + beta * qvec[1])
+    my = sign[1] * (alpha * dvec[3] + beta * qvec[3])
+    out_ref[...] = jnp.stack([mx, my], axis=1).astype(BF16)
     good = (s >= CLOSE * dd) & (curve >= CLOSE * weight) & (s < TOP) & (curve < TOP)
     for value in (dd, dq, qq, qw):
         good = good & (value > 1.0 / TOP) & (value < TOP)
@@ -519,7 +530,7 @@
 
     return pl.pallas_call(
         fast_kernel,
-        out_shape=(jax.ShapeDtypeStruct((2, LOADS, FACE), BF16), jax.ShapeDtypeStruct((1,), jnp.int32)),
+        out_shape=(jax.ShapeDtypeStruct((LOADS, 2, FACE), BF16), jax.ShapeDtypeStruct((1,), jnp.int32)),
         in_specs=[pl.BlockSpec(memory_space=pl.ANY)] * 4,
         out_specs=(pl.BlockSpec(memory_space=pltpu.VMEM), pl.BlockSpec(memory_space=pltpu.SMEM)),
         scratch_shapes=[
@@ -533,6 +544,7 @@
             faces(F32),
             faces(F32),
             faces(F32),
+            pltpu.VMEM((2, LOADS, HALF), F32),
         ]
         + [pltpu.VMEM((size, 2, 128), F32) for size in (NX * NY, 2 * NZ)]
         + [
@@ -552,7 +564,7 @@
     args = (flexibility, loads, sizes, owner)
     result, good = fast(*args)
     result = lax.cond(good[0] > 0, lambda: result, lambda: exact(*args))
-    return result[None, None]
+    return jnp.transpose(result, (1, 0, 2))[None, None]
 
 def solution(mesh):
     return jax.shard_map(

time: 41.5 us -> 41.6 us (level)
  no operation moved by 1% of the time
where the time goes in v4:
time: 41.6 us; the launch traced here: 41.5 us
  Pallas kernels  40.3 us (97%)
  local copies, waits for them, and re-layouts  0.64 us (2%)
  between operations  0.6 us (1%)
    pallas_call x1, Pallas kernels, fast(): pl.pallas_call(fast_kernel, out_shape=(jax.ShapeDtypeStruct((LOADS, 2, FA...  40.3 us

profile of v4, /device:TPU:1, one launch (start us, length us, event | category | flops | bytes accessed | tf_op | source)
XLA Modules:
  0.0 41.5 jit_solution(1477602342798718307)
XLA Ops:
  0.0 0.0 copy-start
  0.0 0.0 copy-start.2
  0.0 0.0 copy-start.1
  0.0 40.3 %fast.1 = (bf16[36,2,384]{2,1,0:T(2,128)(2,1)S(1)}, s32[1]{0:T(128)}) custom-call(bf16[1,1,1536,1536]{3,2,1,0:T(8,128)(2,1)} %flex_hbm.1, bf16[1,1,36,1536]{3,2,1,0:T(8,128)(2,1)} %loads_hbm.1, s32[4,2,192]{2,1,0:T(2,128)} %bitcast.7, s32[4,2,192]{2,1,0:T(2,128)} %bitcast.9), custom_call_target="tpu_custom_call" | custom-call | tf_op jit(solution)/shard_map/fast/pallas_call | solution.py:531
  40.8 0.0 copy-done
  40.8 0.0 copy-done.2
  40.9 0.0 copy-done.1
  40.9 0.6 %copy.8 = bf16[1,1,2,36,384]{4,2,3,1,0:T(2,128)(2,1)} copy(bf16[1,1,2,36,384]{4,2,3,1,0:T(2,128)(2,1)S(1)} %bitcast.6) | data formatting | bytes 110592
  (1 shorter events, 0.0 us)
Async XLA Ops:
  0.0 40.8 %copy-start = (bf16[1,1,36,1536]{3,2,1,0:T(8,128)(2,1)S(1)}, bf16[1,1,36,1536]{3,2,1,0:T(8,128)(2,1)}, u32[]{:S(2)}) copy-start(bf16[1,1,36,1536]{3,2,1,0:T(8,128)(2,1)} %loads_hbm.1) | copy-start | bytes 331780
  0.0 40.8 %copy-start.2 = (s32[192,4,2]{0,2,1:T(2,128)S(1)}, s32[192,4,2]{0,2,1:T(2,128)}, u32[]{:S(2)}) copy-start(s32[192,4,2]{0,2,1:T(2,128)} %param.9) | copy-start | bytes 18436
  0.0 40.8 %copy-start.1 = (s32[192,4,2]{0,2,1:T(2,128)S(1)}, s32[192,4,2]{0,2,1:T(2,128)}, u32[]{:S(2)}) copy-start(s32[192,4,2]{0,2,1:T(2,128)} %param.8) | copy-start | bytes 18436

commit v5 on v3

--- a/solution.py
+++ b/solution.py
@@ -326,7 +326,7 @@
 
 def fast_kernel(
     flex_hbm, loads_hbm, sizes_hbm, owner_hbm, out_ref, good_ref,
-    flex, loads, meta, sign_meta, u0, r0, u1, r1, dvec, qvec,
+    flex, loads, meta, sign_meta, u0, r0, u1, r1, dvec, qvec, low_ref,
     buf0, buf1,
     load_sem, u_sem, sum_sem, word,
 ):
@@ -435,11 +435,12 @@
         return jnp.concatenate(pair, axis=1)
 
     pair = jump(0, copies0, u0, r0, dvec)
-    low = [half_product(pair, 0, half) for half in range(2)]
+    for half in range(2):
+        low_ref[half] = half_product(pair, 0, half)
     pair = jump(1, copies0, u0, r0, dvec)
     copies1 = {}
     for half in (1, 0):
-        value = low[half] + half_product(pair, 1, half)
+        value = low_ref[half] + half_product(pair, 1, half)
         u1[2 * half] = value[:, 0:FACE]
         u1[2 * half + 1] = value[:, FACE:]
         copies1[half] = exchange(1, half, u1, r1)
@@ -447,10 +448,10 @@
     tell(3)
     top = lanes(dvec[1] * dvec[1] + dvec[3] * dvec[3], 0)
     first = jump(0, copies1, u1, r1, qvec)
-    low = [half_product(first, 0, half) for half in range(2)]
+    low_ref[0] = first.astype(F32) * half_product(first, 0, 0)
+    low_ref[1] = 2.0 * half_product(first, 0, 1)
     second = jump(1, copies1, u1, r1, qvec)
-    inner = first.astype(F32) * low[0]
-    inner = inner + second.astype(F32) * (2.0 * low[1] + half_product(second, 1, 1))
+    inner = low_ref[0] + second.astype(F32) * (low_ref[1] + half_product(second, 1, 1))
     top = top + lanes(dvec[1] * qvec[1] + dvec[3] * qvec[3], 64)
     bottom = lanes(qvec[1] * qvec[1] + qvec[3] * qvec[3], 0) + lanes(inner, 64)
     sums = jnp.concatenate([top, bottom], axis=0)
@@ -533,6 +534,7 @@
             faces(F32),
             faces(F32),
             faces(F32),
+            pltpu.VMEM((2, LOADS, HALF), F32),
         ]
         + [pltpu.VMEM((size, 2, 128), F32) for size in (NX * NY, 2 * NZ)]
         + [

time: 41.5 us -> 41.4 us (level)
  no operation moved by 1% of the time
where the time goes in v5:
time: 41.4 us; the launch traced here: 41.3 us
  Pallas kernels  39.8 us (96%)
  between operations  0.74 us (2%)
  local copies, waits for them, and re-layouts  0.67 us (2%)
    pallas_call x1, Pallas kernels, fast(): pl.pallas_call(fast_kernel, out_shape=(jax.ShapeDtypeStruct((2, LOADS, FA...  39.8 us

profile of v5, /device:TPU:1, one launch (start us, length us, event | category | flops | bytes accessed | tf_op | source)
XLA Modules:
  0.0 41.3 jit_solution(12095733064306423151)
XLA Ops:
  0.0 0.0 copy-start
  0.0 0.0 copy-start.3
  0.0 0.0 copy-start.2
  0.0 39.8 %fast.1 = (bf16[2,36,384]{2,1,0:T(8,128)(2,1)S(1)}, s32[1]{0:T(128)}) custom-call(bf16[1,1,1536,1536]{3,2,1,0:T(8,128)(2,1)} %flex_hbm.1, bf16[1,1,36,1536]{3,2,1,0:T(8,128)(2,1)} %loads_hbm.1, s32[4,2,192]{2,1,0:T(2,128)} %bitcast.7, s32[4,2,192]{2,1,0:T(2,128)} %bitcast.9), custom_call_target="tpu_custom_call" | custom-call | tf_op jit(solution)/shard_map/fast/pallas_call | solution.py:521
  40.6 0.0 copy-done
  40.6 0.0 copy-done.3
  40.6 0.0 copy-done.2
  40.6 0.1 conditional.1
  40.7 0.0 copy-start.1
  40.7 0.6 %copy-done.1 = bf16[1,1,2,36,384]{4,2,3,1,0:T(2,128)(2,1)} copy-done((bf16[1,1,2,36,384]{4,2,3,1,0:T(2,128)(2,1)}, bf16[1,1,2,36,384]{4,2,3,1,0:T(2,128)(2,1)S(1)}, u32[]{:S(2)}) %copy-start.1) | copy-done | bytes 55320
  (1 shorter events, 0.0 us)
Async XLA Ops:
  0.0 40.6 %copy-start = (bf16[1,1,36,1536]{3,2,1,0:T(8,128)(2,1)S(1)}, bf16[1,1,36,1536]{3,2,1,0:T(8,128)(2,1)}, u32[]{:S(2)}) copy-start(bf16[1,1,36,1536]{3,2,1,0:T(8,128)(2,1)} %loads_hbm.1) | copy-start | bytes 331780
  0.0 40.6 %copy-start.3 = (s32[192,4,2]{0,2,1:T(2,128)S(1)}, s32[192,4,2]{0,2,1:T(2,128)}, u32[]{:S(2)}) copy-start(s32[192,4,2]{0,2,1:T(2,128)} %param.9) | copy-start | bytes 18436
  0.0 40.6 %copy-start.2 = (s32[192,4,2]{0,2,1:T(2,128)S(1)}, s32[192,4,2]{0,2,1:T(2,128)}, u32[]{:S(2)}) copy-start(s32[192,4,2]{0,2,1:T(2,128)} %param.8) | copy-start | bytes 18436
  40.7 0.6 %copy-start.1 = (bf16[1,1,2,36,384]{4,2,3,1,0:T(2,128)(2,1)}, bf16[1,1,2,36,384]{4,2,3,1,0:T(2,128)(2,1)S(1)}, u32[]{:S(2)}) copy-start(bf16[1,1,2,36,384]{4,2,3,1,0:T(2,128)(2,1)S(1)} %get-tuple-element.31) | copy-start | bytes 165892
